TPU v7x, 128 devices: a whole 4x4x4 slice. The times are simulated.
128 devices in a mesh: quad: 8 (over z, x_lo), row: 16 (over x_hi, y, core).
Axes of the slice: x: 4 (x_hi: 2, x_lo: 2; x = x_hi * 2 + x_lo), y: 4, z: 4, core: 2. Of those that a mesh axis runs over, the one named last changes fastest.
Arguments:
- hamiltonian: bfloat16 [1024, 64, 1536], P('row'), may hold values from -0.15625 to 0.15625
- columns: int32 [1024, 24], P('row'), may hold values from 0 to 1023, as said below
- counts: int32 [1024], P('row'), may hold values from 2 to 24, as said below
- precond: bfloat16 [16, 1024, 64, 128], P('quad', 'row'), may hold values from -0.5 to 0.5
- rhs: bfloat16 [65536, 128], P('row'), may hold values from -6 to 6
Outputs:
- moments_out: float32 [8, 65536, 128], P('quad', 'row')
- blocks_out: float32 [8, 128, 128], P('quad')
Inputs may be any that keep to these rules, and one draw needn't show every extreme that they name: `columns`: slot 0 of row block b holds b itself; slot 1 holds b - 64 for even b and b + 64 for odd b, reflected at the ends (an index -m becomes m, an index 1023 + m becomes 1024 - 1 - m); every column block lies within 64 blocks of its row block. `counts`: every run of 64 row blocks starting at a multiple of 64 holds a row block with all 24 slots live.
All inputs are finite; a program needn't handle non-finite values.
Results may differ from a plain program's by a relative error of at most 0.02.
Values may be sent and summed in bfloat16 or wider, within the bound.
No kernel may reach another device: no remote copies, remote signals or barrier semaphores. Data moves between devices by JAX's collectives and lax.ppermute only.
A program may use at most 128 MiB of HBM per device.

v0:
```python
import math
import jax
import jax.numpy as jnp
from jax import lax
from jax.sharding import PartitionSpec as P

ITERS = 2
MOMENTS = 8


def extended_2(x, sides, width):
    for axis, dim in sides:
        peers, length = (lax.axis_size(axis), x.shape[dim])
        up = [(i, (i + 1) % peers) for i in range(peers - 1)]
        down = [(j, i) for i, j in up]
        last = lax.slice_in_dim(x, length - width, length, axis=dim)
        first = lax.slice_in_dim(x, 0, width, axis=dim)
        before = lax.ppermute(last, axis, up)
        after = lax.ppermute(first, axis, down)
        x = jnp.concatenate([before, x, after], axis=dim)
    return x


def rotate(values):
    half_cols = values.shape[-1] // 2
    return jnp.concatenate([-values[..., half_cols:], values[..., :half_cols]], axis=-1)


def precondition(blocks_pre, resid):
    stacked = jnp.concatenate([resid, rotate(resid)], axis=1)
    return jnp.einsum("bij,bjc->bic", blocks_pre, stacked, preferred_element_type=jnp.float32)


def shards(hamiltonian, columns, counts, precond, rhs):
    row_blocks = hamiltonian.shape[0]
    block_size = hamiltonian.shape[1]
    slots = columns.shape[1]
    width = rhs.shape[1]
    per_quad = precond.shape[0]
    quad_count = lax.axis_size("quad")
    row_count = lax.axis_size("row")
    quads_total = per_quad * quad_count
    per_device = MOMENTS // quad_count
    local_rows = row_blocks * block_size
    row_index = lax.axis_index("row")
    quad_index = lax.axis_index("quad")
    first_block = (row_index - 1) * row_blocks
    live = jnp.arange(slots)[None, :] < counts[:, None]
    local_index = jnp.where(live, columns - first_block, 3 * row_blocks)
    rhs_blocks = rhs.reshape(row_blocks, block_size, width)
    rhs_float = rhs_blocks.astype(jnp.float32)
    thetas = []
    solutions = []
    for which in range(per_quad):
        theta = (
            2.0 * jnp.pi * ((quad_index * per_quad + which).astype(jnp.float32) + 0.5) / quads_total
        )
        thetas.append(theta)
        zreal = jnp.cos(theta)
        zimag = jnp.sin(theta)
        iterate = precondition(precond[which], rhs_blocks).astype(jnp.bfloat16)
        for sweep in range(ITERS):
            flat = iterate.reshape(local_rows, width)
            extended = extended_2(flat, (("row", 0),), local_rows)
            stacked = jnp.concatenate(
                [
                    extended.reshape(3 * row_blocks, block_size, width),
                    jnp.zeros((1, block_size, width), jnp.bfloat16),
                ],
                axis=0,
            )
            gathered = stacked[local_index].reshape(row_blocks, slots * block_size, width)
            product = jnp.einsum(
                "bij,bjc->bic", hamiltonian, gathered, preferred_element_type=jnp.float32
            )
            current = iterate.astype(jnp.float32)
            shifted = zreal * current + zimag * rotate(current)
            resid = (rhs_float - (shifted - product)).astype(jnp.bfloat16)
            iterate = (current + precondition(precond[which], resid)).astype(jnp.bfloat16)
        solutions.append(iterate.reshape(local_rows, width))
    orders = jnp.arange(lax.axis_size("quad") * per_device).astype(jnp.float32) + 1.0
    total = jnp.zeros((lax.axis_size("quad") * per_device, local_rows, width), jnp.float32)
    for which in range(per_quad):
        phase = orders * thetas[which]
        coef_a = jnp.cos(phase) / quads_total
        coef_b = jnp.sin(phase) / quads_total
        current = solutions[which].astype(jnp.float32)
        total = (
            total
            + coef_a[:, None, None] * current[None]
            + coef_b[:, None, None] * rotate(current)[None]
        )
    held = lax.optimization_barrier(total.astype(jnp.bfloat16))
    moments_out = lax.psum_scatter(
        held.astype(jnp.float32).astype(jnp.bfloat16), "quad", scatter_dimension=0, tiled=True
    ).astype(jnp.float32)
    scale = 1.0 / math.sqrt(local_rows * row_count)
    flat_rhs = rhs.astype(jnp.float32)
    local_blocks = (
        jnp.einsum("rc,krd->kcd", flat_rhs, moments_out, precision=lax.Precision.HIGHEST) * scale
    )
    blocks_out = lax.psum(local_blocks.astype(jnp.bfloat16), "row").astype(jnp.float32)
    return (moments_out, blocks_out)


def solution(mesh):
    return jax.shard_map(
        shards,
        mesh=mesh,
        in_specs=(
            P("row", None, None),
            P("row", None),
            P("row"),
            P("quad", "row", None, None),
            P("row", None),
        ),
        out_specs=(P("quad", "row", None), P("quad", None, None)),
        check_vma=False,
    )
```

profile of v0, /device:TPU:0, one launch (start us, length us, event | category | flops | bytes accessed | tf_op | source)
XLA Modules:
  0.0 562.5 jit_solution(10902191708547151597)
XLA Ops:
  7.2 2.1 slice_negate_fusion.10
  9.4 0.4 copy-done.8
  9.8 0.7 bitcast_convert_fusion.1
  10.5 2.5 collective-permute-start.4
  13.0 1.3 collective-permute-start.5
  14.3 2.5 bitcast_convert_fusion.3
  16.8 4.9 collective-permute-start
  21.7 1.3 collective-permute-start.1
  23.3 0.1 copy.8
  23.4 0.1 reshape.108
  23.5 0.6 sine_multiply_fusion
  24.1 0.6 sine_multiply_fusion.1
  24.7 2.8 slice_negate_fusion.2
  27.6 2.8 slice_negate_fusion.5
  30.4 8.6 %pad_maximum_fusion.2 = bf16[12288,128]{1,0:T(8,128)(2,1)S(1)} fusion(bf16[4096,128]{1,0:T(8,128)(2,1)} %collective-permute-done.5, bf16[4096,128]{1,0:T(8,128)(2,1)S(1)} %bitcast.108, bf16[4096,128]{1,0:T(8,128)(2,1)} %collective-permute-done.4), kind=kLoop, calls=%fused_computation.11 | loop fusion | flops 9437184 | bytes 6291456 | tf_op jit(solution)/shard_map/concatenate | solution.py:20
  39.0 0.7 concatenate.89
  39.7 32.0 %gather_fusion.2 = bf16[1536,64,128]{2,1,0:T(8,128)(2,1)} fusion(bf16[193,64,128]{2,1,0:T(8,128)(2,1)S(1)} %concatenate.89, s32[2048]{0:T(1024)S(1)} %pad_clamp_fusion), kind=kCustom, calls=%fused_computation.2 | custom fusion | bytes 50337792 | tf_op jit(solution)/shard_map/gather | solution.py:72
  71.8 16.3 %fusion.2 = bf16[64,64,128]{2,1,0:T(8,128)(2,1)S(1)} fusion(bf16[64,64,128]{2,1,0:T(8,128)(2,1)} %bitcast.100, f32[64,64,64]{2,1,0:T(8,128)} %get-tuple-element.13, f32[64,64,64]{2,1,0:T(8,128)} %get-tuple-element.12, bf16[64,64,1536]{2,1,0:T(8,128)(2,1)} %param.5, bf16[64,1536,128]{2,1,0:T(8,128)(2,1)} %bitcast.97, bf16[64,128,64]{1,2,0:T(8,128)(2,1)} %copy-done.5, ...), kind=kOutput, calls=%fused_computation.15 | convolution fusion | flops 1615331328 | bytes 42991624 | tf_op jit(solution)/shard_map/bij,bjc->bic/dot_general | solution.py:73
  88.1 0.4 slice_negate_fusion.7
  88.5 0.8 copy-done.6
  89.3 0.7 copy-done.9
  90.0 2.6 fusion.71
  92.6 4.3 collective-permute-start.6
  96.9 1.3 collective-permute-start.7
  98.2 4.1 pad_maximum_fusion
  102.4 0.7 concatenate.78
  103.1 32.0 %gather_fusion = bf16[1536,64,128]{2,1,0:T(8,128)(2,1)} fusion(bf16[193,64,128]{2,1,0:T(8,128)(2,1)S(1)} %concatenate.78, s32[2048]{0:T(1024)S(1)} %pad_clamp_fusion), kind=kCustom, calls=%fused_computation | custom fusion | bytes 50337792 | tf_op jit(solution)/shard_map/gather | solution.py:72
  135.1 16.1 %fusion = bf16[64,64,128]{2,1,0:T(8,128)(2,1)S(1)} fusion(bf16[64,64,128]{2,1,0:T(8,128)(2,1)} %bitcast.101, f32[64,64,64]{2,1,0:T(8,128)} %get-tuple-element.9, f32[64,64,64]{2,1,0:T(8,128)} %get-tuple-element.8, bf16[64,64,1536]{2,1,0:T(8,128)(2,1)} %param.5, bf16[64,1536,128]{2,1,0:T(8,128)(2,1)} %bitcast.98, ...), kind=kOutput, calls=%fused_computation.13 | convolution fusion | flops 1615331328 | bytes 42991624 | tf_op jit(solution)/shard_map/bij,bjc->bic/dot_general | solution.py:73
  151.2 0.4 slice_negate_fusion.9
  151.6 3.0 slice.127
  154.6 3.1 fusion.72
  157.7 4.2 collective-permute-start.2
  162.0 1.7 collective-permute-start.3
  163.7 2.8 slice.117
  166.4 1.9 slice_negate_fusion.1
  168.4 2.0 slice_negate_fusion.4
  170.4 4.1 pad_maximum_fusion.3
  174.5 0.7 concatenate.94
  175.2 32.0 %gather_fusion.3 = bf16[1536,64,128]{2,1,0:T(8,128)(2,1)} fusion(bf16[193,64,128]{2,1,0:T(8,128)(2,1)S(1)} %concatenate.94, s32[2048]{0:T(1024)S(1)} %pad_clamp_fusion), kind=kCustom, calls=%fused_computation.3 | custom fusion | bytes 50337792 | tf_op jit(solution)/shard_map/gather | solution.py:72
  207.3 16.1 %fusion.3 = bf16[64,64,128]{2,1,0:T(8,128)(2,1)S(1)} fusion(bf16[64,64,128]{2,1,0:T(8,128)(2,1)} %bitcast.102, f32[64,64,64]{2,1,0:T(8,128)} %slice.127, f32[64,64,64]{2,1,0:T(8,128)} %slice_negate_fusion.1, bf16[64,64,1536]{2,1,0:T(8,128)(2,1)} %param.5, bf16[64,1536,128]{2,1,0:T(8,128)(2,1)} %bitcast.96, bf16[64,64,128]{2,1,0:T(8,128)(2,1)} %get-tuple-element.27, ...), kind=kOutput, calls=%fused_computation.16 | convolution fusion | flops 1615331328 | bytes 42991624 | tf_op jit(solution)/shard_map/bij,bjc->bic/dot_general | solution.py:73
  223.4 0.4 slice_negate_fusion.6
  223.8 1.1 copy-done.11
  225.0 2.1 fusion.36
  227.1 0.2 bitcast_convert_fusion
  227.3 2.7 slice_negate_fusion
  230.0 4.3 pad_maximum_fusion.1
  234.3 0.7 concatenate.83
  235.0 32.0 %gather_fusion.1 = bf16[1536,64,128]{2,1,0:T(8,128)(2,1)} fusion(bf16[193,64,128]{2,1,0:T(8,128)(2,1)S(1)} %concatenate.83, s32[2048]{0:T(1024)S(1)} %pad_clamp_fusion), kind=kCustom, calls=%fused_computation.1 | custom fusion | bytes 50337792 | tf_op jit(solution)/shard_map/gather | solution.py:72
  267.1 16.4 %fusion.1 = bf16[64,64,128]{2,1,0:T(8,128)(2,1)S(1)} fusion(bf16[64,64,128]{2,1,0:T(8,128)(2,1)} %bitcast.103, f32[64,64,64]{2,1,0:T(8,128)} %slice.117, f32[64,64,64]{2,1,0:T(8,128)} %slice_negate_fusion.4, bf16[64,64,1536]{2,1,0:T(8,128)(2,1)} %param.5, bf16[64,1536,128]{2,1,0:T(8,128)(2,1)} %bitcast.95, bf16[64,64,128]{2,1,0:T(8,128)(2,1)} %get-tuple-element.31, ...), kind=kOutput, calls=%fused_computation.14 | convolution fusion | flops 1615331328 | bytes 42991624 | tf_op jit(solution)/shard_map/bij,bjc->bic/dot_general | solution.py:73
  283.5 0.4 slice_negate_fusion.8
  283.9 1.1 copy-done.12
  285.1 2.1 fusion.38
  287.2 0.2 bitcast_convert_fusion.2
  287.4 0.7 slice_negate_fusion.3
  288.1 0.9 copy-done.13
  289.0 0.6 copy-done.14
  289.6 1.1 pad_maximum_fusion.4
  290.8 0.4 copy-done.3
  291.2 6.1 %add_convert_fusion = bf16[8,4096,128]{2,1,0:T(8,128)(2,1)} fusion(f32[4096,128]{1,0:T(8,128)S(1)} %get-tuple-element.37, f32[8]{0:T(128)S(1)} %copy-done.17, f32[4096,128]{1,0:T(8,128)S(1)} %copy-done.3, f32[8]{0:T(128)S(1)} %copy-done.18, f32[4096,128]{1,0:T(8,128)S(1)} %get-tuple-element.36, f32[8]{0:T(128)S(1)} %copy-done.19, ...), kind=kLoop, calls=%fused_computation.4 | loop fusion | flops 33554432 | bytes 16777344 | tf_op jit(solution)/shard_map/convert_element_type | solution.py:93
  297.4 185.1 %reduce-scatter.2.cloned.1.call-done = bf16[1,4096,128]{2,1,0:T(8,128)(2,1)} async-done(((bf16[8,4096,128]{2,1,0:T(8,128)(2,1)}), bf16[1,4096,128]{2,1,0:T(8,128)(2,1)}) %reduce-scatter.2.cloned.1.call-update) | async-done | bytes 1048592 | tf_op jit(solution)/shard_map/reduce_scatter | solution.py:94
  482.4 1.8 fusion.49
  484.2 69.1 %psum.7 = bf16[1,128,128]{1,2,0:T(8,128)(2,1)S(1)} all-reduce(bf16[1,128,128]{1,2,0:T(8,128)(2,1)S(1)} %fusion.49), channel_id=1, replica_groups=mesh['quad'=8,'row'=16] {'row'}, use_global_device_ids=true, to_apply=%region_1.2 | all-reduce | flops 16384 | bytes 65536 | tf_op jit(solution)/shard_map/psum | solution.py:102
  553.3 0.7 copy.9
  554.0 1.5 convert_element_type.141
  (48 shorter events, 0.2 us)
Async XLA Ops:
  7.2 475.2 %reduce-scatter.2.cloned.1.call-start = ((), (), s32[]{:S(2)}) async-start(), calls=%async_computation.1 | async-start | bytes 9437184 | tf_op jit(solution)/shard_map/reduce_scatter | solution.py:94
  7.2 2.2 copy-start
  7.2 2.5 copy-start.8
  10.5 19.9 %copy-start.5 = (bf16[64,128,64]{1,2,0:T(8,128)(2,1)}, bf16[64,128,64]{1,2,0:T(8,128)(2,1)S(1)}, u32[]{:S(2)}) copy-start(bf16[64,128,64]{1,2,0:T(8,128)(2,1)S(1)} %get-tuple-element.25) | copy-start | bytes 3145732
  10.5 12.8 %copy-start.16 = (s32[64,24]{0,1:T(8,128)S(1)}, s32[64,24]{0,1:T(8,128)}, u32[]{:S(2)}) copy-start(s32[64,24]{0,1:T(8,128)} %param.6) | copy-start | bytes 18436
  10.5 12.8 %copy-start.21 = (s32[64]{0:T(128)S(1)}, s32[64]{0:T(128)}, u32[]{:S(2)}) copy-start(s32[64]{0:T(128)} %param.7) | copy-start | bytes 772
  10.5 19.8 %collective-permute-start.4 = (bf16[4096,128]{1,0:T(8,128)(2,1)S(1)}, bf16[4096,128]{1,0:T(8,128)(2,1)}, u32[]{:S(2)}, u32[]{:S(2)}) collective-permute-start(bf16[4096,128]{1,0:T(8,128)(2,1)S(1)} %bitcast.106), channel_id=1, source_target_pairs={{0,1},{1,2},{2,3},{3,4},{4,5},{5,6},{6,7},{7,8},{8,9},{9,10},{10,1... | collective-permute-start | bytes 3145736 | tf_op jit(solution)/shard_map/ppermute | solution.py:18
  13.0 17.4 %collective-permute-start.5 = (bf16[4096,128]{1,0:T(8,128)(2,1)S(1)}, bf16[4096,128]{1,0:T(8,128)(2,1)}, u32[]{:S(2)}, u32[]{:S(2)}) collective-permute-start(bf16[4096,128]{1,0:T(8,128)(2,1)S(1)} %bitcast.107), channel_id=1, source_target_pairs={{1,0},{2,1},{3,2},{4,3},{5,4},{6,5},{7,6},{8,7},{9,8},{10,9},{11,1... | collective-permute-start | bytes 3145736 | tf_op jit(solution)/shard_map/ppermute | solution.py:19
  16.8 81.4 %collective-permute-start = (bf16[4096,128]{1,0:T(8,128)(2,1)}, bf16[4096,128]{1,0:T(8,128)(2,1)}, u32[]{:S(2)}, u32[]{:S(2)}) collective-permute-start(bf16[4096,128]{1,0:T(8,128)(2,1)} %bitcast.3), channel_id=1, source_target_pairs={{0,1},{1,2},{2,3},{3,4},{4,5},{5,6},{6,7},{7,8},{8,9},{9,10},{10,1... | collective-permute-start | bytes 3145736 | tf_op jit(solution)/shard_map/ppermute | solution.py:18
  21.7 76.5 %collective-permute-start.1 = (bf16[4096,128]{1,0:T(8,128)(2,1)}, bf16[4096,128]{1,0:T(8,128)(2,1)}, u32[]{:S(2)}, u32[]{:S(2)}) collective-permute-start(bf16[4096,128]{1,0:T(8,128)(2,1)} %bitcast.3), channel_id=1, source_target_pairs={{1,0},{2,1},{3,2},{4,3},{5,4},{6,5},{7,6},{8,7},{9,8},{10,9},{11,1... | collective-permute-start | bytes 3145736 | tf_op jit(solution)/shard_map/ppermute | solution.py:19
  24.7 2.8 copy-start.4
  88.1 1.2 copy-start.6
  88.1 1.9 copy-start.9
  92.6 77.8 %collective-permute-start.6 = (bf16[4096,128]{1,0:T(8,128)(2,1)}, bf16[4096,128]{1,0:T(8,128)(2,1)}, u32[]{:S(2)}, u32[]{:S(2)}) collective-permute-start(bf16[4096,128]{1,0:T(8,128)(2,1)} %bitcast.24), channel_id=1, source_target_pairs={{0,1},{1,2},{2,3},{3,4},{4,5},{5,6},{6,7},{7,8},{8,9},{9,10},{10,1... | collective-permute-start | bytes 3145736 | tf_op jit(solution)/shard_map/ppermute | solution.py:18
  96.9 73.5 %collective-permute-start.7 = (bf16[4096,128]{1,0:T(8,128)(2,1)}, bf16[4096,128]{1,0:T(8,128)(2,1)}, u32[]{:S(2)}, u32[]{:S(2)}) collective-permute-start(bf16[4096,128]{1,0:T(8,128)(2,1)} %bitcast.24), channel_id=1, source_target_pairs={{1,0},{2,1},{3,2},{4,3},{5,4},{6,5},{7,6},{8,7},{9,8},{10,9},{11,1... | collective-permute-start | bytes 3145736 | tf_op jit(solution)/shard_map/ppermute | solution.py:19
  151.6 3.0 copy-start.10
  157.7 8.7 %copy-start.7 = (f32[64,64,128]{2,1,0:T(8,128)S(1)}, f32[64,64,128]{2,1,0:T(8,128)}, u32[]{:S(2)}) copy-start(f32[64,64,128]{2,1,0:T(8,128)} %get-tuple-element.26) | copy-start | bytes 6291460
  157.7 72.3 %collective-permute-start.2 = (bf16[4096,128]{1,0:T(8,128)(2,1)}, bf16[4096,128]{1,0:T(8,128)(2,1)}, u32[]{:S(2)}, u32[]{:S(2)}) collective-permute-start(bf16[4096,128]{1,0:T(8,128)(2,1)} %bitcast.9), channel_id=1, source_target_pairs={{0,1},{1,2},{2,3},{3,4},{4,5},{5,6},{6,7},{7,8},{8,9},{9,10},{10,1... | collective-permute-start | bytes 3145736 | tf_op jit(solution)/shard_map/ppermute | solution.py:18
  162.0 68.0 %collective-permute-start.3 = (bf16[4096,128]{1,0:T(8,128)(2,1)}, bf16[4096,128]{1,0:T(8,128)(2,1)}, u32[]{:S(2)}, u32[]{:S(2)}) collective-permute-start(bf16[4096,128]{1,0:T(8,128)(2,1)} %bitcast.9), channel_id=1, source_target_pairs={{1,0},{2,1},{3,2},{4,3},{5,4},{6,5},{7,6},{8,7},{9,8},{10,9},{11,1... | collective-permute-start | bytes 3145736 | tf_op jit(solution)/shard_map/ppermute | solution.py:19
  223.4 1.6 copy-start.11
  227.3 2.7 copy-start.2
  283.5 1.6 copy-start.12
  287.4 1.6 copy-start.13
  287.4 2.2 copy-start.14
  289.6 1.6 copy-start.3
  289.6 1.6 copy-start.17
  289.6 1.6 copy-start.18
  289.6 1.6 copy-start.19
  289.6 1.6 copy-start.20
  297.3 185.1 %copy-start.1 = (bf16[4096,128]{1,0:T(8,128)(2,1)S(1)}, bf16[4096,128]{1,0:T(8,128)(2,1)}, u32[]{:S(2)}) copy-start(bf16[4096,128]{1,0:T(8,128)(2,1)} %param.9) | copy-start | bytes 3145732
  482.4 71.6 %copy-start.15 = (bf16[1,4096,128]{2,1,0:T(8,128)(2,1)S(1)}, bf16[1,4096,128]{2,1,0:T(8,128)(2,1)}, u32[]{:S(2)}) copy-start(bf16[1,4096,128]{2,1,0:T(8,128)(2,1)} %reduce-scatter.2.cloned.1.call-done) | copy-start | bytes 3145732
Sparse Core Ops, SparseCore 0:
  297.5 184.8 reduce-scatter.1
where the time goes:
time: 567 us; the launch traced here: 563 us
  waiting for transfers between devices  185 us (33%)
  local copies, waits for them, and re-layouts  144 us (25%)
  matrix products  79.8 us (14%)
  blocking collectives  69.1 us (12%)
  other arithmetic  48.4 us (9%)
  starting transfers between devices  21.5 us (4%)
  between operations  15 us (3%)
    reduce_scatter x1, waiting for transfers between devices, shards(): lax.psum_scatter(held.astype(jnp.float32).astype(jnp.bfloat16), 'quad', s...  185 us
    gather x4, local copies, waits for them, and re-layouts, shards(): stacked[local_index].reshape(row_blocks, slots * block_size, width)  128 us
    psum x1, blocking collectives, shards(): lax.psum(local_blocks.astype(jnp.bfloat16), 'row').astype(jnp.float32)  69.1 us
    dot_general x4, matrix products, shards(): jnp.einsum('bij,bjc->bic', hamiltonian, gathered, preferred_element_type=...  64.9 us
    concatenate x4, other arithmetic, extended_2(): x = jnp.concatenate([before, x, after], axis=dim)  21.2 us
    neg x11, other arithmetic, rotate(): -values[..., half_cols:]  16.8 us
    ppermute x4, starting transfers between devices, extended_2(): before = lax.ppermute(last, axis, up)  15.9 us
    dot_general x6, matrix products, precondition(): jnp.einsum('bij,bjc->bic', blocks_pre, stacked, preferred_element_type=jn...  13.1 us
  transfers between devices with their start and end apart: 9, of which 1 were waited for; matrix products, arithmetic and copies ran while one was open for 35% of the time, Pallas kernels for 0%

commit v1 on v0

--- a/solution.py
+++ b/solution.py
@@ -99,7 +99,9 @@
     local_blocks = (
         jnp.einsum("rc,krd->kcd", flat_rhs, moments_out, precision=lax.Precision.HIGHEST) * scale
     )
-    blocks_out = lax.psum(local_blocks.astype(jnp.bfloat16), "row").astype(jnp.float32)
+    blocks_out = jnp.sum(lax.all_gather(local_blocks.astype(jnp.bfloat16), "row"), axis=0).astype(
+        jnp.float32
+    )
     return (moments_out, blocks_out)
 
 

time: 567 us -> 524 us (0.924)
  blocking collectives: 69.1 us -> 25.2 us
    psum x1 -> x0, blocking collectives: 69.1 us -> none  [shards(): lax.psum(local_blocks.astype(jnp.bfloat16), 'row').astype(jnp.float32)]
    all_gather x0 -> x1, blocking collectives: none -> 25.2 us  [shards(): lax.all_gather(local_blocks.astype(jnp.bfloat16), 'row')]
  transfers between devices with their start and end apart: 9 -> 9, of which waited for: 1 -> 1; matrix products, arithmetic and copies ran while one was open for 35% -> 38% of each run, Pallas kernels for 0% -> 0%
where the time goes in v1:
time: 524 us; the launch traced here: 519 us
  waiting for transfers between devices  185 us (35%)
  local copies, waits for them, and re-layouts  144 us (27%)
  matrix products  79.8 us (15%)
  other arithmetic  48.5 us (9%)
  blocking collectives  25.2 us (5%)
  starting transfers between devices  21.5 us (4%)
  between operations  15 us (3%)
    reduce_scatter x1, waiting for transfers between devices, shards(): lax.psum_scatter(held.astype(jnp.float32).astype(jnp.bfloat16), 'quad', s...  185 us
    gather x4, local copies, waits for them, and re-layouts, shards(): stacked[local_index].reshape(row_blocks, slots * block_size, width)  128 us
    dot_general x4, matrix products, shards(): jnp.einsum('bij,bjc->bic', hamiltonian, gathered, preferred_element_type=...  64.9 us
    all_gather x1, blocking collectives, shards(): lax.all_gather(local_blocks.astype(jnp.bfloat16), 'row')  25.2 us
    concatenate x4, other arithmetic, extended_2(): x = jnp.concatenate([before, x, after], axis=dim)  21.2 us
    neg x11, other arithmetic, rotate(): -values[..., half_cols:]  16.8 us
    ppermute x4, starting transfers between devices, extended_2(): before = lax.ppermute(last, axis, up)  15.9 us
    dot_general x6, matrix products, precondition(): jnp.einsum('bij,bjc->bic', blocks_pre, stacked, preferred_element_type=jn...  13.1 us
  transfers between devices with their start and end apart: 9, of which 1 were waited for; matrix products, arithmetic and copies ran while one was open for 38% of the time, Pallas kernels for 0%

profile of v1, /device:TPU:0, one launch (start us, length us, event | category | flops | bytes accessed | tf_op | source)
XLA Modules:
  0.0 519.0 jit_solution(16007697086097431848)
XLA Ops:
  7.2 2.1 slice_negate_fusion.10
  9.4 0.4 copy-done.8
  9.8 0.7 bitcast_convert_fusion.1
  10.5 2.5 collective-permute-start.4
  13.0 1.3 collective-permute-start.5
  14.3 2.5 bitcast_convert_fusion.3
  16.8 4.9 collective-permute-start
  21.7 1.3 collective-permute-start.1
  23.5 0.6 sine_multiply_fusion
  24.1 0.6 sine_multiply_fusion.1
  24.7 2.8 slice_negate_fusion.2
  27.6 2.8 slice_negate_fusion.5
  30.4 8.6 %pad_maximum_fusion.2 = bf16[12288,128]{1,0:T(8,128)(2,1)S(1)} fusion(bf16[4096,128]{1,0:T(8,128)(2,1)} %collective-permute-done.5, bf16[4096,128]{1,0:T(8,128)(2,1)S(1)} %bitcast.111, bf16[4096,128]{1,0:T(8,128)(2,1)} %collective-permute-done.4), kind=kLoop, calls=%fused_computation.11 | loop fusion | flops 9437184 | bytes 6291456 | tf_op jit(solution)/shard_map/concatenate | solution.py:20
  39.0 0.7 concatenate.89
  39.7 32.0 %gather_fusion.2 = bf16[1536,64,128]{2,1,0:T(8,128)(2,1)} fusion(bf16[193,64,128]{2,1,0:T(8,128)(2,1)S(1)} %concatenate.89, s32[2048]{0:T(1024)S(1)} %pad_clamp_fusion), kind=kCustom, calls=%fused_computation.2 | custom fusion | bytes 50337792 | tf_op jit(solution)/shard_map/gather | solution.py:72
  71.8 16.3 %fusion.2 = bf16[64,64,128]{2,1,0:T(8,128)(2,1)S(1)} fusion(bf16[64,64,128]{2,1,0:T(8,128)(2,1)} %bitcast.103, f32[64,64,64]{2,1,0:T(8,128)} %get-tuple-element.11, f32[64,64,64]{2,1,0:T(8,128)} %get-tuple-element.10, bf16[64,64,1536]{2,1,0:T(8,128)(2,1)} %param.5, bf16[64,1536,128]{2,1,0:T(8,128)(2,1)} %bitcast.100, bf16[64,128,64]{1,2,0:T(8,128)(2,1)} %copy-done.5, ...), kind=kOutput, calls=%fused_computation.15 | convolution fusion | flops 1615331328 | bytes 42991624 | tf_op jit(solution)/shard_map/bij,bjc->bic/dot_general | solution.py:73
  88.1 0.4 slice_negate_fusion.7
  88.5 0.8 copy-done.6
  89.3 0.7 copy-done.9
  90.0 2.6 fusion.71
  92.6 4.3 collective-permute-start.6
  96.9 1.3 collective-permute-start.7
  98.2 4.1 pad_maximum_fusion
  102.4 0.7 concatenate.78
  103.1 32.0 %gather_fusion = bf16[1536,64,128]{2,1,0:T(8,128)(2,1)} fusion(bf16[193,64,128]{2,1,0:T(8,128)(2,1)S(1)} %concatenate.78, s32[2048]{0:T(1024)S(1)} %pad_clamp_fusion), kind=kCustom, calls=%fused_computation | custom fusion | bytes 50337792 | tf_op jit(solution)/shard_map/gather | solution.py:72
  135.1 16.1 %fusion = bf16[64,64,128]{2,1,0:T(8,128)(2,1)S(1)} fusion(bf16[64,64,128]{2,1,0:T(8,128)(2,1)} %bitcast.104, f32[64,64,64]{2,1,0:T(8,128)} %get-tuple-element.7, f32[64,64,64]{2,1,0:T(8,128)} %get-tuple-element.6, bf16[64,64,1536]{2,1,0:T(8,128)(2,1)} %param.5, bf16[64,1536,128]{2,1,0:T(8,128)(2,1)} %bitcast.101, ...), kind=kOutput, calls=%fused_computation.13 | convolution fusion | flops 1615331328 | bytes 42991624 | tf_op jit(solution)/shard_map/bij,bjc->bic/dot_general | solution.py:73
  151.2 0.4 slice_negate_fusion.9
  151.6 3.0 slice.127
  154.6 3.1 fusion.72
  157.7 4.2 collective-permute-start.2
  162.0 1.7 collective-permute-start.3
  163.7 2.8 slice.117
  166.4 1.9 slice_negate_fusion.1
  168.4 2.0 slice_negate_fusion.4
  170.4 4.1 pad_maximum_fusion.3
  174.5 0.7 concatenate.94
  175.2 32.0 %gather_fusion.3 = bf16[1536,64,128]{2,1,0:T(8,128)(2,1)} fusion(bf16[193,64,128]{2,1,0:T(8,128)(2,1)S(1)} %concatenate.94, s32[2048]{0:T(1024)S(1)} %pad_clamp_fusion), kind=kCustom, calls=%fused_computation.3 | custom fusion | bytes 50337792 | tf_op jit(solution)/shard_map/gather | solution.py:72
  207.3 16.1 %fusion.3 = bf16[64,64,128]{2,1,0:T(8,128)(2,1)S(1)} fusion(bf16[64,64,128]{2,1,0:T(8,128)(2,1)} %bitcast.105, f32[64,64,64]{2,1,0:T(8,128)} %slice.127, f32[64,64,64]{2,1,0:T(8,128)} %slice_negate_fusion.1, bf16[64,64,1536]{2,1,0:T(8,128)(2,1)} %param.5, bf16[64,1536,128]{2,1,0:T(8,128)(2,1)} %bitcast.99, bf16[64,64,128]{2,1,0:T(8,128)(2,1)} %get-tuple-element.25, ...), kind=kOutput, calls=%fused_computation.16 | convolution fusion | flops 1615331328 | bytes 42991624 | tf_op jit(solution)/shard_map/bij,bjc->bic/dot_general | solution.py:73
  223.4 0.4 slice_negate_fusion.6
  223.8 1.1 copy-done.11
  225.0 2.1 fusion.36
  227.1 0.2 bitcast_convert_fusion
  227.3 2.7 slice_negate_fusion
  230.0 4.3 pad_maximum_fusion.1
  234.3 0.7 concatenate.83
  235.0 32.0 %gather_fusion.1 = bf16[1536,64,128]{2,1,0:T(8,128)(2,1)} fusion(bf16[193,64,128]{2,1,0:T(8,128)(2,1)S(1)} %concatenate.83, s32[2048]{0:T(1024)S(1)} %pad_clamp_fusion), kind=kCustom, calls=%fused_computation.1 | custom fusion | bytes 50337792 | tf_op jit(solution)/shard_map/gather | solution.py:72
  267.1 16.4 %fusion.1 = bf16[64,64,128]{2,1,0:T(8,128)(2,1)S(1)} fusion(bf16[64,64,128]{2,1,0:T(8,128)(2,1)} %bitcast.106, f32[64,64,64]{2,1,0:T(8,128)} %slice.117, f32[64,64,64]{2,1,0:T(8,128)} %slice_negate_fusion.4, bf16[64,64,1536]{2,1,0:T(8,128)(2,1)} %param.5, bf16[64,1536,128]{2,1,0:T(8,128)(2,1)} %bitcast.98, bf16[64,64,128]{2,1,0:T(8,128)(2,1)} %get-tuple-element.29, ...), kind=kOutput, calls=%fused_computation.14 | convolution fusion | flops 1615331328 | bytes 42991624 | tf_op jit(solution)/shard_map/bij,bjc->bic/dot_general | solution.py:73
  283.5 0.4 slice_negate_fusion.8
  283.9 1.1 copy-done.12
  285.1 2.1 fusion.38
  287.2 0.2 bitcast_convert_fusion.2
  287.4 0.7 slice_negate_fusion.3
  288.1 0.9 copy-done.13
  289.0 0.6 copy-done.14
  289.6 1.1 pad_maximum_fusion.4
  290.8 0.4 copy-done.3
  291.2 6.1 %add_convert_fusion = bf16[8,4096,128]{2,1,0:T(8,128)(2,1)} fusion(f32[4096,128]{1,0:T(8,128)S(1)} %get-tuple-element.35, f32[8]{0:T(128)S(1)} %copy-done.17, f32[4096,128]{1,0:T(8,128)S(1)} %copy-done.3, f32[8]{0:T(128)S(1)} %copy-done.18, f32[4096,128]{1,0:T(8,128)S(1)} %get-tuple-element.34, f32[8]{0:T(128)S(1)} %copy-done.19, ...), kind=kLoop, calls=%fused_computation.4 | loop fusion | flops 33554432 | bytes 16777344 | tf_op jit(solution)/shard_map/convert_element_type | solution.py:93
  297.4 185.1 %reduce-scatter.2.cloned.1.call-done = bf16[1,4096,128]{2,1,0:T(8,128)(2,1)} async-done(((bf16[8,4096,128]{2,1,0:T(8,128)(2,1)}), bf16[1,4096,128]{2,1,0:T(8,128)(2,1)}) %reduce-scatter.2.cloned.1.call-update) | async-done | bytes 1048592 | tf_op jit(solution)/shard_map/reduce_scatter | solution.py:94
  482.4 1.8 fusion.49
  484.2 0.1 copy.9
  484.3 25.2 %all-gather = bf16[16,128,128]{2,1,0:T(8,128)(2,1)S(1)} all-gather(bf16[1,128,128]{2,1,0:T(8,128)(2,1)S(1)} %copy.9), channel_id=2, replica_groups=mesh['quad'=8,'row'=16] {'row'}, dimensions={0}, use_global_device_ids=true | all-gather | bytes 557056 | tf_op jit(solution)/shard_map/all_gather | solution.py:102
  509.6 0.1 copy.12
  509.7 0.7 copy.11
  510.5 1.5 convert_element_type.154
  (52 shorter events, 0.4 us)
Async XLA Ops:
  7.2 475.2 %reduce-scatter.2.cloned.1.call-start = ((), (), s32[]{:S(2)}) async-start(), calls=%async_computation.1 | async-start | bytes 9437184 | tf_op jit(solution)/shard_map/reduce_scatter | solution.py:94
  7.2 2.2 copy-start
  7.2 2.5 copy-start.8
  10.5 19.9 %copy-start.5 = (bf16[64,128,64]{1,2,0:T(8,128)(2,1)}, bf16[64,128,64]{1,2,0:T(8,128)(2,1)S(1)}, u32[]{:S(2)}) copy-start(bf16[64,128,64]{1,2,0:T(8,128)(2,1)S(1)} %get-tuple-element.23) | copy-start | bytes 3145732
  10.5 12.8 %copy-start.16 = (s32[64,24]{0,1:T(8,128)S(1)}, s32[64,24]{0,1:T(8,128)}, u32[]{:S(2)}) copy-start(s32[64,24]{0,1:T(8,128)} %param.6) | copy-start | bytes 18436
  10.5 12.8 %copy-start.21 = (s32[64]{0:T(128)S(1)}, s32[64]{0:T(128)}, u32[]{:S(2)}) copy-start(s32[64]{0:T(128)} %param.7) | copy-start | bytes 772
  10.5 19.8 %collective-permute-start.4 = (bf16[4096,128]{1,0:T(8,128)(2,1)S(1)}, bf16[4096,128]{1,0:T(8,128)(2,1)}, u32[]{:S(2)}, u32[]{:S(2)}) collective-permute-start(bf16[4096,128]{1,0:T(8,128)(2,1)S(1)} %bitcast.109), channel_id=1, source_target_pairs={{0,1},{1,2},{2,3},{3,4},{4,5},{5,6},{6,7},{7,8},{8,9},{9,10},{10,1... | collective-permute-start | bytes 3145736 | tf_op jit(solution)/shard_map/ppermute | solution.py:18
  13.0 17.4 %collective-permute-start.5 = (bf16[4096,128]{1,0:T(8,128)(2,1)S(1)}, bf16[4096,128]{1,0:T(8,128)(2,1)}, u32[]{:S(2)}, u32[]{:S(2)}) collective-permute-start(bf16[4096,128]{1,0:T(8,128)(2,1)S(1)} %bitcast.110), channel_id=1, source_target_pairs={{1,0},{2,1},{3,2},{4,3},{5,4},{6,5},{7,6},{8,7},{9,8},{10,9},{11,1... | collective-permute-start | bytes 3145736 | tf_op jit(solution)/shard_map/ppermute | solution.py:19
  16.8 81.4 %collective-permute-start = (bf16[4096,128]{1,0:T(8,128)(2,1)}, bf16[4096,128]{1,0:T(8,128)(2,1)}, u32[]{:S(2)}, u32[]{:S(2)}) collective-permute-start(bf16[4096,128]{1,0:T(8,128)(2,1)} %bitcast.3), channel_id=1, source_target_pairs={{0,1},{1,2},{2,3},{3,4},{4,5},{5,6},{6,7},{7,8},{8,9},{9,10},{10,1... | collective-permute-start | bytes 3145736 | tf_op jit(solution)/shard_map/ppermute | solution.py:18
  21.7 76.5 %collective-permute-start.1 = (bf16[4096,128]{1,0:T(8,128)(2,1)}, bf16[4096,128]{1,0:T(8,128)(2,1)}, u32[]{:S(2)}, u32[]{:S(2)}) collective-permute-start(bf16[4096,128]{1,0:T(8,128)(2,1)} %bitcast.3), channel_id=1, source_target_pairs={{1,0},{2,1},{3,2},{4,3},{5,4},{6,5},{7,6},{8,7},{9,8},{10,9},{11,1... | collective-permute-start | bytes 3145736 | tf_op jit(solution)/shard_map/ppermute | solution.py:19
  24.7 2.8 copy-start.4
  88.1 1.2 copy-start.6
  88.1 1.9 copy-start.9
  92.6 77.8 %collective-permute-start.6 = (bf16[4096,128]{1,0:T(8,128)(2,1)}, bf16[4096,128]{1,0:T(8,128)(2,1)}, u32[]{:S(2)}, u32[]{:S(2)}) collective-permute-start(bf16[4096,128]{1,0:T(8,128)(2,1)} %bitcast.24), channel_id=1, source_target_pairs={{0,1},{1,2},{2,3},{3,4},{4,5},{5,6},{6,7},{7,8},{8,9},{9,10},{10,1... | collective-permute-start | bytes 3145736 | tf_op jit(solution)/shard_map/ppermute | solution.py:18
  96.9 73.5 %collective-permute-start.7 = (bf16[4096,128]{1,0:T(8,128)(2,1)}, bf16[4096,128]{1,0:T(8,128)(2,1)}, u32[]{:S(2)}, u32[]{:S(2)}) collective-permute-start(bf16[4096,128]{1,0:T(8,128)(2,1)} %bitcast.24), channel_id=1, source_target_pairs={{1,0},{2,1},{3,2},{4,3},{5,4},{6,5},{7,6},{8,7},{9,8},{10,9},{11,1... | collective-permute-start | bytes 3145736 | tf_op jit(solution)/shard_map/ppermute | solution.py:19
  151.6 3.0 copy-start.10
  157.7 8.7 %copy-start.7 = (f32[64,64,128]{2,1,0:T(8,128)S(1)}, f32[64,64,128]{2,1,0:T(8,128)}, u32[]{:S(2)}) copy-start(f32[64,64,128]{2,1,0:T(8,128)} %get-tuple-element.24) | copy-start | bytes 6291460
  157.7 72.3 %collective-permute-start.2 = (bf16[4096,128]{1,0:T(8,128)(2,1)}, bf16[4096,128]{1,0:T(8,128)(2,1)}, u32[]{:S(2)}, u32[]{:S(2)}) collective-permute-start(bf16[4096,128]{1,0:T(8,128)(2,1)} %bitcast.9), channel_id=1, source_target_pairs={{0,1},{1,2},{2,3},{3,4},{4,5},{5,6},{6,7},{7,8},{8,9},{9,10},{10,1... | collective-permute-start | bytes 3145736 | tf_op jit(solution)/shard_map/ppermute | solution.py:18
  162.0 68.0 %collective-permute-start.3 = (bf16[4096,128]{1,0:T(8,128)(2,1)}, bf16[4096,128]{1,0:T(8,128)(2,1)}, u32[]{:S(2)}, u32[]{:S(2)}) collective-permute-start(bf16[4096,128]{1,0:T(8,128)(2,1)} %bitcast.9), channel_id=1, source_target_pairs={{1,0},{2,1},{3,2},{4,3},{5,4},{6,5},{7,6},{8,7},{9,8},{10,9},{11,1... | collective-permute-start | bytes 3145736 | tf_op jit(solution)/shard_map/ppermute | solution.py:19
  223.4 1.6 copy-start.11
  227.3 2.7 copy-start.2
  283.5 1.6 copy-start.12
  287.4 1.6 copy-start.13
  287.4 2.2 copy-start.14
  289.6 1.6 copy-start.3
  289.6 1.6 copy-start.17
  289.6 1.6 copy-start.18
  289.6 1.6 copy-start.19
  289.6 1.6 copy-start.20
  297.3 185.1 %copy-start.1 = (bf16[4096,128]{1,0:T(8,128)(2,1)S(1)}, bf16[4096,128]{1,0:T(8,128)(2,1)}, u32[]{:S(2)}) copy-start(bf16[4096,128]{1,0:T(8,128)(2,1)} %param.9) | copy-start | bytes 3145732
  482.4 28.1 %copy-start.15 = (bf16[1,4096,128]{2,1,0:T(8,128)(2,1)S(1)}, bf16[1,4096,128]{2,1,0:T(8,128)(2,1)}, u32[]{:S(2)}) copy-start(bf16[1,4096,128]{2,1,0:T(8,128)(2,1)} %reduce-scatter.2.cloned.1.call-done) | copy-start | bytes 3145732
Sparse Core Ops, SparseCore 0:
  297.5 184.8 reduce-scatter.1
